TPU v7x, 512 devices: a whole 4x8x8 slice. The times are simulated.
512 devices in a mesh: batch: 4 (over x_hi, core), space: 128 (over x_lo, y, z).
Axes of the slice: x: 4 (x_hi: 2, x_lo: 2; x = x_hi * 2 + x_lo), y: 8, z: 8, core: 2. Of those that a mesh axis runs over, the one named last changes fastest.
Arguments:
- inputs: bfloat16 [4, 32, 128, 128, 128], P('batch', None, None, 'space'), may hold values from -6 to 6
- pre_act: bfloat16 [4, 32, 128, 128, 128], P('batch', None, None, 'space'), may hold values from -8 to 8
- cotangent: bfloat16 [4, 32, 128, 128, 128], P('batch', None, None, 'space'), may hold values from -6 to 6
- spectral_weight: bfloat16 [2, 32, 32, 16384], P(None, None, None, 'space'), may hold values from -6 to 6
- skip_weight: bfloat16 [32, 32], replicated, may hold values from -1 to 1
Outputs:
- grad_inputs: bfloat16 [4, 32, 128, 128, 128], P('batch', None, None, 'space')
- grad_spectral: float32 [2, 32, 32, 16384], P(None, None, 'batch', 'space')
- grad_skip: float32 [32, 32], replicated
All inputs are finite; a program needn't handle non-finite values.
Results may differ from a plain program's by a relative error of at most 0.0055.
Values sent between devices are 32-bit elements; how exact they have to be, the bound alone decides.
A program may use at most 64 MiB of HBM per device.

v0:
```python
import math
import jax
import jax.numpy as jnp
from jax import lax
from jax.sharding import PartitionSpec as P

NX = 128
NY = 128
NZ = 128
MX = 16
MY = 16
MZ = 16
HIGHEST = lax.Precision.HIGHEST


def phase_table(length, count, signed):
    points = jnp.arange(length, dtype=jnp.int32)
    orders = jnp.arange(count, dtype=jnp.int32)
    if signed:
        orders = jnp.where(orders < count // 2, orders, orders - count)
    residues = jnp.mod(points[:, None] * orders[None, :], length)
    radians = residues.astype(jnp.float32) * (2.0 * math.pi / length)
    return (jnp.cos(radians), jnp.sin(radians))


def forward_block(cosine, sine):
    return jnp.stack(
        [jnp.stack([cosine, -sine], axis=1), jnp.stack([sine, cosine], axis=1)], axis=0
    )


def inverse_block(cosine, sine):
    cos_rows = cosine.T
    sin_rows = sine.T
    return jnp.stack(
        [jnp.stack([cos_rows, sin_rows], axis=1), jnp.stack([-sin_rows, cos_rows], axis=1)], axis=0
    )


def gelu_slope(values):
    normal_cdf = 0.5 * (1.0 + jax.scipy.special.erf(values * (1.0 / math.sqrt(2.0))))
    density = jnp.exp(-0.5 * values * values) * (1.0 / math.sqrt(2.0 * math.pi))
    return normal_cdf + values * density


def local_spectrum(grid_in):
    cos_x, sin_x = phase_table(NX, 2 * MX, True)
    table_x = jnp.stack([cos_x, -sin_x], axis=1).astype(jnp.bfloat16)
    section_x = jnp.einsum(
        "scxyz,xpa->scpayz", grid_in, table_x, preferred_element_type=jnp.float32
    )
    cos_z, sin_z = phase_table(NZ, MZ, False)
    section_z = jnp.einsum(
        "scpayz,pzqk->scqyak", section_x, forward_block(cos_z, sin_z), precision=HIGHEST
    )
    return section_z.reshape(
        section_z.shape[0], section_z.shape[1], 2, section_z.shape[3], 2 * MX * MZ
    )


def along_y(spectra):
    cos_y, sin_y = phase_table(NY, 2 * MY, True)
    section_y = jnp.einsum(
        "scpym,pyqk->scqmk", spectra, forward_block(cos_y, sin_y), precision=HIGHEST
    )
    return section_y.reshape(section_y.shape[0], section_y.shape[1], 2, section_y.shape[3] * 2 * MY)


def both_along_y(spectra_pair):
    return (along_y(spectra_pair[0]), along_y(spectra_pair[1]))


def to_grid(spectra):
    shaped = spectra.reshape(spectra.shape[0], spectra.shape[1], 2, spectra.shape[3], 2 * MX, MZ)
    cos_z, sin_z = phase_table(NZ, MZ, False)
    grid_z = jnp.einsum(
        "scpyak,pkqz->scqayz", shaped, inverse_block(cos_z, sin_z), precision=HIGHEST
    )
    cos_x, sin_x = phase_table(NX, 2 * MX, True)
    table_x = jnp.stack([cos_x.T, -sin_x.T], axis=0)
    return jnp.einsum("scpayz,pax->scxyz", grid_z, table_x, precision=HIGHEST)


def cross_terms(spec_left, spec_right):
    real_part = jnp.einsum(
        "sim,som->iom", spec_left[:, :, 0], spec_right[:, :, 0], precision=HIGHEST
    )
    real_part = real_part + jnp.einsum(
        "sim,som->iom", spec_left[:, :, 1], spec_right[:, :, 1], precision=HIGHEST
    )
    imag_part = jnp.einsum(
        "sim,som->iom", spec_left[:, :, 0], spec_right[:, :, 1], precision=HIGHEST
    )
    imag_part = imag_part - jnp.einsum(
        "sim,som->iom", spec_left[:, :, 1], spec_right[:, :, 0], precision=HIGHEST
    )
    return jnp.stack([real_part, imag_part], axis=0)


def contract(weight_part, spec_part):
    return jnp.einsum("iom,som->sim", weight_part, spec_part, preferred_element_type=jnp.float32)


def skip_gradient(grid_in, cot_pre):
    partial_sum = jnp.einsum(
        "sixyz,soxyz->io", grid_in, cot_pre, preferred_element_type=jnp.float32
    )
    summed = lax.psum(partial_sum, ("batch", "space"))
    return summed / math.sqrt(grid_in.shape[0] * lax.axis_size("batch") * NX * NY * NZ)


def on_device(inputs, pre_act, cotangent, spectral_weight, skip_weight):
    samples = inputs.shape[0]
    channels = inputs.shape[1]
    slope_pre = gelu_slope(pre_act.astype(jnp.float32))
    cot_pre = (cotangent.astype(jnp.float32) * slope_pre).astype(jnp.bfloat16)
    spec_u, spec_e = both_along_y(
        (
            lax.all_to_all(
                local_spectrum(inputs), "space", split_axis=4, concat_axis=3, tiled=True
            ),
            lax.all_to_all(
                local_spectrum(cot_pre), "space", split_axis=4, concat_axis=3, tiled=True
            ),
        )
    )
    mode_count = spec_u.shape[3]
    position = jnp.arange(mode_count, dtype=jnp.int32)
    kxz_index = lax.axis_index("space") * (mode_count // (2 * MY)) + position // (2 * MY)
    mode_weights = jnp.where(kxz_index % MZ == 0, 1.0, 2.0).astype(jnp.float32) / float(
        NX * NY * NZ
    )
    mode_grad = lax.psum_scatter(
        cross_terms(spec_u, spec_e), "batch", scatter_dimension=2, tiled=True
    )
    grad_spectral = mode_grad * mode_weights
    rounded = spec_e.astype(jnp.bfloat16)
    weight_real = spectral_weight[0]
    weight_imag = spectral_weight[1]
    back_real = contract(weight_real, rounded[:, :, 0]) + contract(weight_imag, rounded[:, :, 1])
    back_imag = contract(weight_real, rounded[:, :, 1]) - contract(weight_imag, rounded[:, :, 0])
    back_modes = jnp.stack([back_real, back_imag], axis=2) * mode_weights
    shaped = back_modes.reshape(samples, channels, 2, mode_count // (2 * MY), 2 * MY)
    cos_y, sin_y = phase_table(NY, 2 * MY, True)
    grid_y = jnp.einsum("scpmk,pkqy->scqym", shaped, inverse_block(cos_y, sin_y), precision=HIGHEST)
    spatial = to_grid(lax.all_to_all(grid_y, "space", split_axis=3, concat_axis=4, tiled=True))
    mixed = jnp.einsum("io,soxyz->sixyz", skip_weight, cot_pre, preferred_element_type=jnp.float32)
    grad_inputs = (spatial + mixed).astype(jnp.bfloat16)
    grad_skip = skip_gradient(inputs, cot_pre)
    return (grad_inputs, grad_spectral, grad_skip)


def solution(mesh):
    placed = (
        P("batch", None, None, "space", None),
        P("batch", None, None, "space", None),
        P("batch", None, None, "space", None),
        P(None, None, None, "space"),
        P(),
    )
    return jax.shard_map(
        on_device,
        mesh=mesh,
        in_specs=placed,
        out_specs=(P("batch", None, None, "space", None), P(None, None, "batch", "space"), P()),
        check_vma=False,
    )
```

profile of v0, /device:TPU:2, one launch (start us, length us, event | category | flops | bytes accessed | tf_op | source)
XLA Modules:
  0.0 209.4 jit_solution(695585654018447)
XLA Ops:
  7.2 0.0 copy-start
  7.2 0.1 fusion.89
  7.3 0.1 fusion.84
  7.3 0.2 fusion.73
  7.5 2.3 %fusion.8 = bf16[1,32,128,1,128]{4,2,3,1,0:T(8,128)(2,1)S(1)} fusion(bf16[1,32,128,1,128]{4,2,3,1,0:T(8,128)(2,1)} %param.6, bf16[1,32,128,1,128]{4,2,3,1,0:T(8,128)(2,1)} %param.7), kind=kLoop, calls=%fused_computation.13 | loop fusion | flops 6291456 | bytes 3145728 | tf_op jit(solution)/shard_map/convert_element_type | solution.py:116
  9.8 0.3 convolution_bitcast_fusion.2
  10.1 2.5 %convolution_bitcast_fusion.4 = f32[1,32,2,1,32,16]{4,5,1,2,3,0:T(8,128)S(1)} fusion(f32[32,2,32,128]{3,2,0,1:T(8,128)S(1)} %convolution_bitcast_fusion.2, f32[1,128,2,16]{1,3,0,2:T(8,128)S(1)} %get-tuple-element.33, f32[1,128,2,16]{1,3,0,2:T(8,128)S(1)} %get-tuple-element.32), kind=kOutput, calls=%fused_computation.19 | convolution fusion | flops 100671488 | bytes 1212416 | tf_op jit(solution)/shard_map/scpayz,pzqk->scqyak/dot_general | solution.py:53
  12.6 0.4 copy.55
  12.9 0.4 copy.162
  13.3 1.2 reshape.693
  14.5 18.7 %all-to-all-start = ((f32[128,1,256]{2,1,0:T(1,128)}), f32[128,1,256]{2,1,0:T(1,128)S(1)}, u32[]{:S(2)}, u32[]{:S(2)}) async-start(f32[128,1,256]{2,1,0:T(1,128)} %reshape.693), calls=%async_computation | async-start | bytes 262144 | tf_op jit(solution)/shard_map/all_to_all | solution.py:122
  33.2 0.1 fusion.88
  33.3 0.1 fusion.86
  33.4 0.2 fusion.75
  33.5 0.0 copy-done
  33.6 0.3 convolution_bitcast_fusion.1
  33.9 0.0 copy-start.3
  33.9 2.5 %convolution_bitcast_fusion.3 = f32[1,32,2,1,32,16]{4,5,1,2,3,0:T(8,128)S(1)} fusion(f32[32,2,32,128]{3,2,0,1:T(8,128)S(1)} %convolution_bitcast_fusion.1, f32[1,128,2,16]{1,3,0,2:T(8,128)S(1)} %get-tuple-element.33, f32[1,128,2,16]{1,3,0,2:T(8,128)S(1)} %get-tuple-element.32), kind=kOutput, calls=%fused_computation.18 | convolution fusion | flops 100671488 | bytes 1212416 | tf_op jit(solution)/shard_map/scpayz,pzqk->scqyak/dot_general | solution.py:53
  36.4 1.3 convolution_bitcast_fusion.6
  37.7 2.1 fusion.18
  39.8 0.4 copy.69
  40.1 0.4 copy.161
  40.5 1.2 reshape.697
  41.7 96.8 %psum.7 = f32[32,32]{0,1:T(8,128)S(1)} all-reduce(f32[32,32]{0,1:T(8,128)S(1)} %convolution_bitcast_fusion.6), channel_id=1, replica_groups=mesh['batch'=4,'space'=128] {'batch','space'}, use_global_device_ids=true, to_apply=%region_1.2 | all-reduce | flops 1024 | bytes 8192 | tf_op jit(solution)/shard_map/psum | solution.py:108
  138.6 0.0 all-to-all-done
  138.6 11.8 %all-to-all-start.2 = ((f32[128,1,256]{2,1,0:T(1,128)}), f32[128,1,256]{2,1,0:T(1,128)S(1)}, u32[]{:S(2)}, u32[]{:S(2)}) async-start(f32[128,1,256]{2,1,0:T(1,128)} %reshape.697), calls=%async_computation.2 | async-start | bytes 262144 | tf_op jit(solution)/shard_map/all_to_all | solution.py:119
  150.4 0.0 reduce-scatter.2.cloned.1.call-start
  150.4 0.5 broadcast.824
  150.9 0.9 reduce.8
  151.9 0.4 reshape.694
  152.3 0.3 copy.59
  152.6 0.5 fusion.28
  153.1 0.1 copy.67
  153.2 0.1 copy.75
  153.2 9.8 %all-to-all-done.2 = f32[128,1,256]{2,1,0:T(1,128)S(1)} async-done(((f32[128,1,256]{2,1,0:T(1,128)}), f32[128,1,256]{2,1,0:T(1,128)S(1)}, u32[]{:S(2)}, u32[]{:S(2)}) %all-to-all-start.2) | async-done | bytes 131104 | tf_op jit(solution)/shard_map/all_to_all | solution.py:119
  163.0 0.9 reduce.10
  163.9 0.4 reshape.698
  164.4 0.3 copy.73
  164.7 0.5 fusion.25
  165.2 0.1 copy.74
  165.2 0.1 copy.76
  165.3 0.2 add_bitcast_fusion
  165.5 0.0 copy-start.2
  165.5 1.1 pad_maximum_fusion
  166.6 0.0 reduce-scatter.2.cloned.1.call-update
  166.6 0.1 copy.130
  166.7 0.1 copy.131
  166.8 0.4 fusion.22
  167.2 0.1 stack.145
  167.3 0.1 stack.144
  167.5 0.3 convolution_bitcast_fusion.5
  167.8 0.3 copy.61
  168.1 1.0 reshape.695
  169.1 7.0 %all-to-all-start.1 = ((f32[128,1,256]{2,1,0:T(1,128)}), f32[128,1,256]{2,1,0:T(1,128)S(1)}, u32[]{:S(2)}, u32[]{:S(2)}) async-start(f32[128,1,256]{2,1,0:T(1,128)} %reshape.695), calls=%async_computation.1 | async-start | bytes 262144 | tf_op jit(solution)/shard_map/all_to_all | solution.py:146
  176.2 0.7 copy.80
  176.8 0.2 fusion.79
  177.0 11.7 %all-to-all-done.1 = f32[128,1,256]{2,1,0:T(1,128)S(1)} async-done(((f32[128,1,256]{2,1,0:T(1,128)}), f32[128,1,256]{2,1,0:T(1,128)S(1)}, u32[]{:S(2)}, u32[]{:S(2)}) %all-to-all-start.1) | async-done | bytes 131104 | tf_op jit(solution)/shard_map/all_to_all | solution.py:146
  188.7 0.9 reduce.9
  189.7 1.0 reshape.696
  190.7 1.9 copy.62
  192.6 2.3 %copy.63 = f32[32,2,32,16]{2,3,1,0:T(8,128)} copy(f32[32,2,32,16]{0,3,2,1:T(8,128)} %bitcast.256) | data formatting | bytes 262144 | tf_op jit(solution)/shard_map/reshape.31
  194.9 2.1 convolution_bitcast_fusion
  197.0 3.9 %fusion.9 = bf16[1,32,128,1,128]{4,2,3,1,0:T(8,128)(2,1)} fusion(f32[128,128,32]{1,2,0:T(8,128)S(1)} %copy-done.1, f32[32,2,32,128]{3,2,0,1:T(8,128)S(1)} %convolution_bitcast_fusion, f32[1,32,128]{2,1,0:T(8,128)S(1)} %get-tuple-element.35, f32[1,32,128]{2,1,0:T(8,128)S(1)} %get-tuple-element.34), kind=kOutput, calls=%fused_computation.15 | convolution fusion | flops 403709952 | bytes 4227072 | tf_op jit(solution)/shard_map/scpayz,pax->scxyz/dot_general | solution.py:81
  200.9 1.7 broadcast_multiply_fusion
  (20 shorter events, 0.2 us)
Async XLA Ops:
  7.2 26.4 %copy-start = (bf16[1,32,128,1,128]{4,2,3,1,0:T(8,128)(2,1)S(1)}, bf16[1,32,128,1,128]{4,2,3,1,0:T(8,128)(2,1)}, u32[]{:S(2)}) copy-start(bf16[1,32,128,1,128]{4,2,3,1,0:T(8,128)(2,1)} %param.5) | copy-start | bytes 3145732
  14.5 124.0 %all-to-all-start = ((f32[128,1,256]{2,1,0:T(1,128)}), f32[128,1,256]{2,1,0:T(1,128)S(1)}, u32[]{:S(2)}, u32[]{:S(2)}) async-start(f32[128,1,256]{2,1,0:T(1,128)} %reshape.693), calls=%async_computation | async-start | bytes 262144 | tf_op jit(solution)/shard_map/all_to_all | solution.py:122
  33.9 3.8 %copy-start.3 = (bf16[32,32]{1,0:T(8,128)(2,1)S(1)}, bf16[32,32]{1,0:T(8,128)(2,1)}, u32[]{:S(2)}) copy-start(bf16[32,32]{1,0:T(8,128)(2,1)} %param.9) | copy-start | bytes 6148
  138.6 24.4 %all-to-all-start.2 = ((f32[128,1,256]{2,1,0:T(1,128)}), f32[128,1,256]{2,1,0:T(1,128)S(1)}, u32[]{:S(2)}, u32[]{:S(2)}) async-start(f32[128,1,256]{2,1,0:T(1,128)} %reshape.697), calls=%async_computation.2 | async-start | bytes 262144 | tf_op jit(solution)/shard_map/all_to_all | solution.py:119
  150.4 50.5 %reduce-scatter.2.cloned.1.call-start = ((), (), s32[]{:S(2)}) async-start(), calls=%async_computation.4 | async-start | bytes 1310720 | tf_op jit(solution)/shard_map/reduce_scatter | solution.py:133
  165.5 1.3 copy-start.2
  169.1 19.6 %all-to-all-start.1 = ((f32[128,1,256]{2,1,0:T(1,128)}), f32[128,1,256]{2,1,0:T(1,128)S(1)}, u32[]{:S(2)}, u32[]{:S(2)}) async-start(f32[128,1,256]{2,1,0:T(1,128)} %reshape.695), calls=%async_computation.1 | async-start | bytes 262144 | tf_op jit(solution)/shard_map/all_to_all | solution.py:146
  189.7 7.3 %copy-start.1 = (f32[128,128,32]{1,2,0:T(8,128)S(1)}, f32[128,128,32]{1,2,0:T(8,128)}, u32[]{:S(2)}) copy-start(f32[128,128,32]{1,2,0:T(8,128)} %fusion.18) | copy-start | bytes 6291460
Sparse Core Ops, SparseCore 0:
  166.7 31.4 reduce-scatter.1
where the time goes:
time: 210 us; the launch traced here: 209 us
  blocking collectives  96.8 us (46%)
  starting transfers between devices  37.6 us (18%)
  waiting for transfers between devices  21.5 us (10%)
  matrix products  16.1 us (8%)
  between operations  14.4 us (7%)
  local copies, waits for them, and re-layouts  13.7 us (7%)
  other arithmetic  9.26 us (4%)
    psum x1, blocking collectives, skip_gradient(): summed = lax.psum(partial_sum, ('batch', 'space'))  96.8 us
    all_to_all x1, starting transfers between devices, on_device(): lax.all_to_all(local_spectrum(cot_pre), 'space', split_axis=4, concat_axi...  18.7 us
    all_to_all x1, starting transfers between devices, on_device(): lax.all_to_all(local_spectrum(inputs), 'space', split_axis=4, concat_axis...  11.8 us
    all_to_all x1, waiting for transfers between devices, on_device(): lax.all_to_all(grid_y, 'space', split_axis=3, concat_axis=4, tiled=True)  11.7 us
    all_to_all x1, waiting for transfers between devices, on_device(): lax.all_to_all(local_spectrum(inputs), 'space', split_axis=4, concat_axis...  9.75 us
    all_to_all x1, starting transfers between devices, on_device(): lax.all_to_all(grid_y, 'space', split_axis=3, concat_axis=4, tiled=True)  7.05 us
    unnamed x17, local copies, waits for them, and re-layouts  6.13 us
    dot_general x2, matrix products, local_spectrum(): jnp.einsum('scpayz,pzqk->scqyak', section_x, forward_block(cos_z, sin_z),...  4.95 us
  transfers between devices with their start and end apart: 4, of which 2 were waited for; matrix products, arithmetic and copies ran while one was open for 13% of the time, Pallas kernels for 0%

commit v1 on v0

--- a/solution.py
+++ b/solution.py
@@ -105,7 +105,7 @@
     partial_sum = jnp.einsum(
         "sixyz,soxyz->io", grid_in, cot_pre, preferred_element_type=jnp.float32
     )
-    summed = lax.psum(partial_sum, ("batch", "space"))
+    summed = lax.psum(lax.psum(partial_sum, axis_name="space"), axis_name="batch")
     return summed / math.sqrt(grid_in.shape[0] * lax.axis_size("batch") * NX * NY * NZ)
 
 

time: 210 us -> 732 us (3.49)
  the two profiles are of different devices: /device:TPU:2 before, /device:TPU:1 now
where the time goes in v1:
time: 732 us; the launch traced here: 731 us
  blocking collectives  623 us (85%)
  starting transfers between devices  31.9 us (4%)
  waiting for transfers between devices  23.1 us (3%)
  matrix products  16.1 us (2%)
  between operations  14.4 us (2%)
  local copies, waits for them, and re-layouts  13.7 us (2%)
  other arithmetic  9.02 us (1%)
    psum x1, blocking collectives, skip_gradient(): lax.psum(partial_sum, axis_name='space')  500 us
    psum x1, blocking collectives, skip_gradient(): lax.psum(lax.psum(partial_sum, axis_name='space'), axis_name='batch')  123 us
    all_to_all x1, starting transfers between devices, on_device(): lax.all_to_all(local_spectrum(cot_pre), 'space', split_axis=4, concat_axi...  19.3 us
  transfers between devices with their start and end apart: 4, of which 3 were waited for; matrix products, arithmetic and copies ran while one was open for 4% of the time, Pallas kernels for 0%

profile of v1, /device:TPU:1, one launch (start us, length us, event | category | flops | bytes accessed | tf_op | source)
XLA Modules:
  0.0 731.4 jit_solution(7930233129228965550)
XLA Ops:
  7.2 0.0 copy-start
  7.2 0.1 fusion.89
  7.3 0.1 fusion.84
  7.3 0.2 fusion.73
  7.5 2.3 fusion.8
  9.8 0.3 convolution_bitcast_fusion.2
  10.1 2.5 convolution_bitcast_fusion.4
  12.6 0.4 copy.55
  12.9 0.4 copy.162
  13.3 1.2 reshape.693
  14.5 19.3 %all-to-all-start = ((f32[128,1,256]{2,1,0:T(1,128)}), f32[128,1,256]{2,1,0:T(1,128)S(1)}, u32[]{:S(2)}, u32[]{:S(2)}) async-start(f32[128,1,256]{2,1,0:T(1,128)} %reshape.693), calls=%async_computation | async-start | bytes 262144 | tf_op jit(solution)/shard_map/all_to_all | solution.py:122
  33.8 0.1 fusion.88
  33.9 0.1 fusion.86
  34.0 0.2 fusion.75
  34.1 0.3 convolution_bitcast_fusion.1
  34.4 0.0 copy-start.3
  34.5 2.5 convolution_bitcast_fusion.3
  36.9 1.3 convolution_bitcast_fusion.6
  38.2 2.1 fusion.18
  40.3 0.4 copy.69
  40.7 0.4 copy.161
  41.1 1.2 reshape.697
  42.3 499.8 %psum.14 = f32[32,32]{0,1:T(8,128)S(1)} all-reduce(f32[32,32]{0,1:T(8,128)S(1)} %convolution_bitcast_fusion.6), channel_id=1, replica_groups=mesh['batch'=4,'space'=128] {'space'}, use_global_device_ids=true, to_apply=%region_1.2 | all-reduce | flops 1024 | bytes 8192 | tf_op jit(solution)/shard_map/psum | solution.py:108
  542.1 123.3 %psum.15 = f32[32,32]{0,1:T(8,128)S(1)} all-reduce(f32[32,32]{0,1:T(8,128)S(1)} %psum.14), channel_id=1, replica_groups=mesh['batch'=4,'space'=128] {'batch'}, use_global_device_ids=true, to_apply=%region_2.3 | all-reduce | flops 1024 | bytes 8192 | tf_op jit(solution)/shard_map/psum | solution.py:108
  665.5 6.2 all-to-all-start.2
  671.7 0.0 reduce-scatter.2.cloned.1.call-start
  671.7 0.5 broadcast.824
  672.2 0.8 reduce.8
  673.0 0.4 reshape.694
  673.5 0.3 copy.59
  673.8 0.5 fusion.28
  674.3 0.1 copy.67
  674.3 0.1 copy.75
  674.4 9.6 %all-to-all-done.2 = f32[128,1,256]{2,1,0:T(1,128)S(1)} async-done(((f32[128,1,256]{2,1,0:T(1,128)}), f32[128,1,256]{2,1,0:T(1,128)S(1)}, u32[]{:S(2)}, u32[]{:S(2)}) %all-to-all-start.2) | async-done | bytes 131104 | tf_op jit(solution)/shard_map/all_to_all | solution.py:119
  684.0 0.8 reduce.10
  684.8 0.4 reshape.698
  685.3 0.3 copy.73
  685.6 0.5 fusion.25
  686.1 0.1 copy.74
  686.1 0.1 copy.76
  686.2 0.2 add_bitcast_fusion
  686.4 0.0 copy-start.2
  686.4 1.1 pad_maximum_fusion
  687.4 0.0 reduce-scatter.2.cloned.1.call-update
  687.5 0.1 copy.130
  687.6 0.1 copy.131
  687.7 0.4 fusion.22
  688.1 0.1 stack.145
  688.2 0.1 stack.144
  688.4 0.3 convolution_bitcast_fusion.5
  688.7 0.3 copy.61
  689.0 1.0 reshape.695
  690.0 6.4 all-to-all-start.1
  696.4 0.7 copy.80
  697.1 0.2 fusion.79
  697.2 11.2 %all-to-all-done.1 = f32[128,1,256]{2,1,0:T(1,128)S(1)} async-done(((f32[128,1,256]{2,1,0:T(1,128)}), f32[128,1,256]{2,1,0:T(1,128)S(1)}, u32[]{:S(2)}, u32[]{:S(2)}) %all-to-all-start.1) | async-done | bytes 131104 | tf_op jit(solution)/shard_map/all_to_all | solution.py:146
  708.5 0.8 reduce.9
  709.3 1.0 reshape.696
  710.4 1.9 copy.62
  712.3 2.3 copy.63
  714.6 2.1 convolution_bitcast_fusion
  716.7 3.9 fusion.9
  720.6 2.3 reduce-scatter.2.cloned.1.call-done
  722.9 1.7 broadcast_multiply_fusion
  (21 shorter events, 0.2 us)
Async XLA Ops:
  7.2 27.0 %copy-start = (bf16[1,32,128,1,128]{4,2,3,1,0:T(8,128)(2,1)S(1)}, bf16[1,32,128,1,128]{4,2,3,1,0:T(8,128)(2,1)}, u32[]{:S(2)}) copy-start(bf16[1,32,128,1,128]{4,2,3,1,0:T(8,128)(2,1)} %param.5) | copy-start | bytes 3145732
  14.5 650.9 %all-to-all-start = ((f32[128,1,256]{2,1,0:T(1,128)}), f32[128,1,256]{2,1,0:T(1,128)S(1)}, u32[]{:S(2)}, u32[]{:S(2)}) async-start(f32[128,1,256]{2,1,0:T(1,128)} %reshape.693), calls=%async_computation | async-start | bytes 262144 | tf_op jit(solution)/shard_map/all_to_all | solution.py:122
  34.4 3.8 copy-start.3
  665.5 18.5 %all-to-all-start.2 = ((f32[128,1,256]{2,1,0:T(1,128)}), f32[128,1,256]{2,1,0:T(1,128)S(1)}, u32[]{:S(2)}, u32[]{:S(2)}) async-start(f32[128,1,256]{2,1,0:T(1,128)} %reshape.697), calls=%async_computation.2 | async-start | bytes 262144 | tf_op jit(solution)/shard_map/all_to_all | solution.py:119
  671.7 51.2 %reduce-scatter.2.cloned.1.call-start = ((), (), s32[]{:S(2)}) async-start(), calls=%async_computation.4 | async-start | bytes 1310720 | tf_op jit(solution)/shard_map/reduce_scatter | solution.py:133
  686.4 1.3 copy-start.2
  690.0 18.5 %all-to-all-start.1 = ((f32[128,1,256]{2,1,0:T(1,128)}), f32[128,1,256]{2,1,0:T(1,128)S(1)}, u32[]{:S(2)}, u32[]{:S(2)}) async-start(f32[128,1,256]{2,1,0:T(1,128)} %reshape.695), calls=%async_computation.1 | async-start | bytes 262144 | tf_op jit(solution)/shard_map/all_to_all | solution.py:146
  709.3 7.4 %copy-start.1 = (f32[128,128,32]{1,2,0:T(8,128)S(1)}, f32[128,128,32]{1,2,0:T(8,128)}, u32[]{:S(2)}) copy-start(f32[128,128,32]{1,2,0:T(8,128)} %fusion.18) | copy-start | bytes 6291460
Sparse Core Ops, SparseCore 0:
  687.6 35.2 reduce-scatter.1
